TPU v7x, 256 devices: a whole 4x4x8 slice. The times are simulated.
256 devices in a mesh: dp: 32 (over x, z), expert: 8 (over y, core).
Axes of the slice: x: 4, y: 4, z: 8, core: 2. Of those that a mesh axis runs over, the one named last changes fastest.
Arguments:
- tokens: bfloat16 [4096, 4096], P('dp', 'expert'), may hold values from -6 to 6
- expert_ids: int32 [4096, 8], P('dp'), may hold values from 0 to 31, all different within a row; in each aligned block of 128 rows (0 to 127, 128 to 255, ...) at most 40 rows name the same one
- scores: float32 [4096, 8], P('dp'), may hold values from 0.05 to 1
- weight_in: bfloat16 [32, 4096, 2048], P('dp', 'expert'), may hold values from -0.09375 to 0.09375
- weight_out: bfloat16 [32, 1024, 4096], P('dp', None, 'expert'), may hold values from -0.1875 to 0.1875
- out_grad: bfloat16 [4096, 4096], P('dp', 'expert'), may hold values from -6 to 6
Outputs:
- layer_out: bfloat16 [4096, 4096], P('dp', 'expert')
- tokens_grad: bfloat16 [4096, 4096], P('dp', 'expert')
- scores_grad: float32 [4096, 8], P('dp')
- w_in_grad: bfloat16 [32, 4096, 2048], P('dp', 'expert')
- w_out_grad: bfloat16 [32, 1024, 4096], P('dp', None, 'expert')
Inputs may be any that keep to these rules, and one draw needn't show every extreme that they name: `expert_ids`: the 8 experts of a token differ. Among the 128 consecutive tokens of one index of dp no expert is named by more than 40 choices, and in every draw some such block names some expert exactly 40 times.
All inputs are finite; a program needn't handle non-finite values.
Results may differ from a plain program's by a relative error of at most 0.0064.
Values may be sent and summed in bfloat16 or wider, within the bound.
No kernel may reach another device: no remote copies, remote signals or barrier semaphores. Data moves between devices by JAX's collectives and lax.ppermute only.
A program may use at most 128 MiB of HBM per device.

v0:
```python
import jax
import jax.numpy as jnp
from jax import lax
from jax.sharding import PartitionSpec as P


ROUTE_SCALE = 2.5
BF = jnp.bfloat16
F32 = jnp.float32


def permute_y(v, step, n_y):
    return lax.ppermute(
        v, "expert", [(2 * y + c, 2 * ((y + step) % n_y) + c) for y in range(n_y) for c in range(2)]
    )


def permute_core(v, n_y):
    return lax.ppermute(
        v, "expert", [(2 * y + c, 2 * y + 1 - c) for y in range(n_y) for c in range(2)]
    )


def dot(a, b):
    return jnp.dot(a, b, preferred_element_type=F32)


def dot_t(a, b):
    return jnp.einsum("rd,fd->rf", a, b, preferred_element_type=F32)


def gather_dot(a, b):
    return jnp.einsum("rd,rf->df", a, b, preferred_element_type=F32)


def reduce_rows(product, own, part, w_own, w_part, n_y):
    rows = own.shape[0] // n_y
    far = (product(own[rows:], w_own) + product(part[rows:], w_part)).astype(BF)
    got = [
        permute_y(far[(d - 1) * rows : d * rows], d, n_y).astype(F32) for d in range(1, n_y)
    ]
    total = product(own[:rows], w_own) + product(part[:rows], w_part)
    for piece in got:
        total = total + piece
    return total


def gather_rows(v, n_y):
    return jnp.concatenate([v] + [permute_y(v, -d, n_y) for d in range(1, n_y)], axis=0)


def relative(slab, half, y, n_y):
    rows = slab.shape[0] // (2 * n_y)
    return jnp.concatenate(
        [
            lax.dynamic_slice_in_dim(slab, (half * n_y + (y + d) % n_y) * rows, rows, 0)
            for d in range(n_y)
        ],
        axis=0,
    )


def absolute(part, y, n_y):
    rows = part.shape[0] // n_y
    return jnp.concatenate(
        [lax.dynamic_slice_in_dim(part, ((yy - y) % n_y) * rows, rows, 0) for yy in range(n_y)],
        axis=0,
    )


def both_halves(own, other, core):
    flat = jnp.where(core == 0, jnp.stack([own, other]), jnp.stack([other, own]))
    return flat.reshape(2 * own.shape[0], own.shape[1])


def body(tokens, expert_ids, scores, weight_in, weight_out, out_grad):
    n_data = lax.axis_size("dp")
    n_y = lax.axis_size("expert") // 2
    here = lax.axis_index("expert")
    y, core = lax.div(here, 2), lax.rem(here, 2)
    tok_count, width = tokens.shape
    top_count = expert_ids.shape[1]
    hidden_units = weight_out.shape[1]
    capacity = min(tok_count, 5 * tok_count * top_count // (4 * n_data))
    slots = n_data * capacity

    ids_t = expert_ids.T
    scores_t = scores.T
    score_total = jnp.sum(scores_t, axis=0, keepdims=True)
    weights_t = ROUTE_SCALE * scores_t / score_total
    named = ids_t[:, None, :] == jnp.arange(n_data, dtype=jnp.int32)[None, :, None]
    hot = jnp.sum(named.astype(F32), axis=0)
    weight_of = jnp.sum(jnp.where(named, weights_t[:, None, :], 0.0), axis=0)
    before = (
        jnp.arange(tok_count, dtype=jnp.int32)[:, None] < jnp.arange(tok_count, dtype=jnp.int32)[None, :]
    ).astype(BF)
    rank = dot(hot.astype(BF), before)
    position = jnp.where(hot > 0.0, rank, -1.0).astype(jnp.int32)
    placed = position[:, None, :] == jnp.arange(capacity, dtype=jnp.int32)[None, :, None]
    place = placed.astype(BF).reshape(slots, tok_count)

    token_send = dot(place, tokens).astype(BF)

    def exchange(v):
        v = v.reshape(n_data, capacity, width)
        return lax.all_to_all(v, "dp", split_axis=0, concat_axis=0, tiled=True).reshape(slots, width)

    in_own, out_own = weight_in[0], weight_out[0]
    token_slab = exchange(token_send)
    in_part = permute_core(in_own, n_y)
    out_part = permute_core(out_own, n_y)

    weight_place = jnp.where(placed, weight_of[:, None, :], 0.0).reshape(slots, tok_count)
    row_weight = jnp.sum(weight_place, axis=1, keepdims=True)
    grad_rows = dot(place, out_grad)
    grad_send = (row_weight * grad_rows).astype(BF)
    grad_rows = grad_rows.astype(BF)
    token_slab, grad_send, in_part, out_part = lax.optimization_barrier(
        (token_slab, grad_send, in_part, out_part)
    )
    grad_slab = exchange(grad_send)

    tok_part = permute_core(relative(token_slab, 1 - core, y, n_y), n_y)
    tok_own = relative(token_slab, core, y, n_y)
    gate_up = reduce_rows(dot, tok_own, tok_part, in_own, in_part, n_y)
    gate, up = gate_up[:, :hidden_units], gate_up[:, hidden_units:]
    sig = jax.nn.sigmoid(gate)
    hidden = (gate * sig * up).astype(BF)
    hid = gather_rows(hidden, n_y)

    grad_slab, _ = lax.optimization_barrier((grad_slab, hidden))
    grad_part = permute_core(relative(grad_slab, 1 - core, y, n_y), n_y)
    grad_own = relative(grad_slab, core, y, n_y)
    hidden_grad = reduce_rows(dot_t, grad_own, grad_part, out_own, out_part, n_y)
    gate_up_grad = jnp.concatenate(
        [hidden_grad * up * sig * (1.0 + gate * (1.0 - sig)), hidden_grad * gate * sig], axis=1
    ).astype(BF)

    out_other = permute_core(absolute(dot(hid, out_part).astype(BF), y, n_y), n_y)
    out_mine = absolute(dot(hid, out_own).astype(BF), y, n_y)
    expert_out = both_halves(out_mine, out_other, core)
    out_back = exchange(expert_out)

    gug = gather_rows(gate_up_grad, n_y)
    grad_other = permute_core(absolute(dot_t(gug, in_part).astype(BF), y, n_y), n_y)
    grad_mine = absolute(dot_t(gug, in_own).astype(BF), y, n_y)
    choice_grad = both_halves(grad_mine, grad_other, core)
    out_back, choice_grad = lax.optimization_barrier((out_back, choice_grad))
    grad_back = exchange(choice_grad)

    tok_part, tok_own, _ = lax.optimization_barrier((tok_part, tok_own, choice_grad))
    w_out_other = permute_core(gather_dot(hid, grad_part), n_y)
    w_out_grad = (gather_dot(hid, grad_own) + w_out_other).astype(BF)
    w_in_other = permute_core(gather_dot(tok_part, gug), n_y)
    w_in_grad = (gather_dot(tok_own, gug) + w_in_other).astype(BF)

    high = lax.reduce_precision(weight_place, 8, 7)
    low = (weight_place - high).astype(BF)
    high = high.astype(BF)
    layer_out = (gather_dot(high, out_back) + gather_dot(low, out_back)).astype(BF)
    slot_dot = jnp.sum(grad_rows.astype(F32) * out_back.astype(F32), axis=1)
    slot_dot = lax.psum(slot_dot.reshape(n_data, capacity), "expert")
    dot_of = jnp.sum(jnp.where(placed, slot_dot[:, :, None], 0.0), axis=1)
    choice_dot = jnp.sum(jnp.where(named, dot_of[None, :, :], 0.0), axis=1)
    scores_grad = (
        ROUTE_SCALE * choice_dot - jnp.sum(choice_dot * weights_t, axis=0, keepdims=True)
    ) / score_total
    tokens_grad = gather_dot(place, grad_back).astype(BF)
    return layer_out, tokens_grad, scores_grad.T, w_in_grad[None], w_out_grad[None]


def solution(mesh):
    return jax.shard_map(
        body,
        mesh=mesh,
        in_specs=(
            P("dp", "expert"),
            P("dp", None),
            P("dp", None),
            P("dp", "expert", None),
            P("dp", None, "expert"),
            P("dp", "expert"),
        ),
        out_specs=(
            P("dp", "expert"),
            P("dp", "expert"),
            P("dp", None),
            P("dp", "expert", None),
            P("dp", None, "expert"),
        ),
        check_vma=False,
    )
```

profile of v0, /device:TPU:33, one launch (start us, length us, event | category | flops | bytes accessed | tf_op | source)
XLA Modules:
  0.0 260.2 jit_solution(15240485398826322309)
XLA Ops:
  0.6 0.7 reduce_sum.73
  1.4 0.7 divide_bitcast_fusion.1
  2.2 0.7 convert_reduce_fusion
  3.3 0.7 copy-done.8
  4.0 2.6 convolution_convert_fusion
  6.6 10.7 %all-to-all-start = ((bf16[32,40,512]{2,1,0:T(8,128)(2,1)}), bf16[32,40,512]{2,1,0:T(8,128)(2,1)}, u32[]{:S(2)}, u32[]{:S(2)}) async-start(bf16[32,40,512]{2,1,0:T(8,128)(2,1)} %bitcast.4), calls=%async_computation | async-start | bytes 2621440 | tf_op jit(solution)/shard_map/all_to_all | solution.py:106
  17.3 1.3 collective-permute-start
  19.0 0.7 mul.62
  19.7 2.6 multiply_convert_fusion
  22.2 1.8 collective-permute-done.1
  24.0 26.4 %all-to-all-done = bf16[32,40,512]{2,1,0:T(8,128)(2,1)} async-done(((bf16[32,40,512]{2,1,0:T(8,128)(2,1)}), bf16[32,40,512]{2,1,0:T(8,128)(2,1)}, u32[]{:S(2)}, u32[]{:S(2)}) %all-to-all-start) | async-done | bytes 1310752 | tf_op jit(solution)/shard_map/all_to_all | solution.py:106
  50.5 2.3 constant_dynamic-slice_fusion.26
  52.8 0.9 pad_maximum_fusion.2
  53.6 2.0 collective-permute-start.2
  55.6 1.5 copy.14
  57.1 4.9 %all-to-all-start.2 = ((bf16[32,40,512]{2,1,0:T(8,128)(2,1)}), bf16[32,40,512]{2,1,0:T(8,128)(2,1)S(1)}, u32[]{:S(2)}, u32[]{:S(2)}) async-start(bf16[32,40,512]{2,1,0:T(8,128)(2,1)} %bitcast.80), calls=%async_computation.2 | async-start | bytes 2621440 | tf_op jit(solution)/shard_map/all_to_all | solution.py:106
  62.0 2.3 fusion.21
  64.2 3.0 %add_convert_fusion.1 = bf16[480,2048]{1,0:T(8,128)(2,1)S(1)} fusion(f32[480,2048]{1,0:T(8,128)S(1)} %fusion.21, bf16[512,2048]{1,0:T(8,128)(2,1)} %collective-permute-done, bf16[640,512]{1,0:T(8,128)(2,1)} %collective-permute-done.2), kind=kOutput, calls=%fused_computation.1 | convolution fusion | flops 1008599040 | bytes 8486912 | tf_op jit(solution)/shard_map/dot_general | solution.py:25
  67.4 2.8 %collective-permute-start.5 = (bf16[160,2048]{1,0:T(8,128)(2,1)S(1)}, bf16[160,2048]{1,0:T(8,128)(2,1)S(1)}, u32[]{:S(2)}, u32[]{:S(2)}) collective-permute-start(bf16[160,2048]{1,0:T(8,128)(2,1)S(1)} %get-tuple-element.28), channel_id=1, source_target_pairs={{0,6},{1,7},{2,0},{3,1},{4,2},{5,3},{6,4},{7,5},{8,14},{9,15},{10,... | collective-permute-start | bytes 1966088 | tf_op jit(solution)/shard_map/ppermute | solution.py:13
  70.6 0.7 collective-permute-start.3
  71.3 2.2 fusion.35
  73.5 24.2 %collective-permute-done.5 = bf16[160,2048]{1,0:T(8,128)(2,1)S(1)} collective-permute-done((bf16[160,2048]{1,0:T(8,128)(2,1)S(1)}, bf16[160,2048]{1,0:T(8,128)(2,1)S(1)}, u32[]{:S(2)}, u32[]{:S(2)}) %collective-permute-start.5) | collective-permute-done | bytes 655392 | tf_op jit(solution)/shard_map/ppermute | solution.py:13
  97.7 4.8 %collective-permute-done.3 = bf16[160,2048]{1,0:T(8,128)(2,1)S(1)} collective-permute-done((bf16[160,2048]{1,0:T(8,128)(2,1)S(1)}, bf16[160,2048]{1,0:T(8,128)(2,1)S(1)}, u32[]{:S(2)}, u32[]{:S(2)}) %collective-permute-start.3) | collective-permute-done | bytes 655392 | tf_op jit(solution)/shard_map/ppermute | solution.py:13
  102.4 0.8 fusion.3
  103.3 1.1 copy-done.4
  104.4 0.9 multiply_convert_fusion.3
  105.3 0.4 collective-permute-start.7
  105.7 2.2 collective-permute-start.6
  108.0 14.6 %collective-permute-done.8 = bf16[160,1024]{1,0:T(8,128)(2,1)} collective-permute-done((bf16[160,1024]{1,0:T(8,128)(2,1)}, bf16[160,1024]{1,0:T(8,128)(2,1)}, u32[]{:S(2)}, u32[]{:S(2)}) %collective-permute-start.8) | collective-permute-done | bytes 327712 | tf_op jit(solution)/shard_map/ppermute | solution.py:13
  123.0 2.5 convolution_convert_fusion.3
  125.5 0.9 pad_maximum_fusion.3
  126.4 1.6 collective-permute-start.9
  128.0 0.8 constant_dynamic-slice_fusion.14
  128.9 2.5 convolution_convert_fusion.4
  131.6 1.9 fusion.27
  133.5 2.2 add_convert_fusion.3
  135.7 1.0 fusion.51
  136.7 2.1 collective-permute-start.13
  138.8 0.6 collective-permute-start.11
  139.4 2.6 maximum_select_fusion
  141.9 9.2 %all-to-all-start.1 = ((bf16[32,40,512]{2,1,0:T(8,128)(2,1)}), bf16[32,40,512]{2,1,0:T(8,128)(2,1)S(1)}, u32[]{:S(2)}, u32[]{:S(2)}) async-start(bf16[32,40,512]{2,1,0:T(8,128)(2,1)} %bitcast.81), calls=%async_computation.1 | async-start | bytes 2621440 | tf_op jit(solution)/shard_map/all_to_all | solution.py:106
  151.2 1.8 fusion.42
  153.0 3.6 %collective-permute-done.11 = bf16[160,1024]{1,0:T(8,128)(2,1)} collective-permute-done((bf16[160,1024]{1,0:T(8,128)(2,1)}, bf16[160,1024]{1,0:T(8,128)(2,1)}, u32[]{:S(2)}, u32[]{:S(2)}) %collective-permute-start.11) | collective-permute-done | bytes 327712 | tf_op jit(solution)/shard_map/ppermute | solution.py:13
  156.7 2.6 %multiply_convert_fusion.2 = (bf16[160,1024]{1,0:T(8,128)(2,1)S(1)}, bf16[160,1024]{1,0:T(8,128)(2,1)S(1)}) fusion(f32[160,2048]{1,0:T(8,128)} %copy-done.4, bf16[160,1024]{1,0:T(8,128)(2,1)} %collective-permute-done.13, bf16[160,1024]{1,0:T(8,128)(2,1)} %collective-permute-done.12, bf16[160,1024]{1,0:T(8,128)(2,1)} %collective-permute-done.11, ...), kind=kOutput, calls=%fused_computation.53 | convolution fusion | flops 171048960 | bytes 4816896 | tf_op jit(solution)/shard_map/rd,fd->rf/dot_general | solution.py:29
  159.5 1.0 collective-permute-start.15
  160.5 1.7 collective-permute-start.14
  162.2 0.9 pad_maximum_fusion.7
  163.0 27.2 %collective-permute-done.16 = bf16[160,2048]{1,0:T(8,128)(2,1)S(1)} collective-permute-done((bf16[160,2048]{1,0:T(8,128)(2,1)S(1)}, bf16[160,2048]{1,0:T(8,128)(2,1)S(1)}, u32[]{:S(2)}, u32[]{:S(2)}) %collective-permute-start.16) | collective-permute-done | bytes 655392 | tf_op jit(solution)/shard_map/ppermute | solution.py:13
  190.6 3.4 %convolution_convert_fusion.1 = bf16[640,512]{1,0:T(8,128)(2,1)S(1)} fusion(bf16[512,2048]{1,0:T(8,128)(2,1)} %collective-permute-done, bf16[160,2048]{1,0:T(8,128)(2,1)S(1)} %collective-permute-done.16, bf16[160,2048]{1,0:T(8,128)(2,1)S(1)} %collective-permute-done.15, bf16[160,2048]{1,0:T(8,128)(2,1)S(1)} %collective-permute-done.14, ...), kind=kOutput, calls=%fused_computation.14 | convolution fusion | flops 1355612160 | bytes 5373952 | tf_op jit(solution)/shard_map/rd,fd->rf/dot_general | solution.py:29
  194.2 2.1 collective-permute-start.17
  196.3 1.6 convolution_convert_fusion.2
  198.0 1.3 maximum_select_fusion.1
  199.4 5.3 %fusion.49 = f32[512,2048]{1,0:T(8,128)} fusion(bf16[640,512]{1,0:T(8,128)(2,1)} %collective-permute-done.2, bf16[160,2048]{1,0:T(8,128)(2,1)S(1)} %copy-done.36, bf16[160,2048]{1,0:T(8,128)(2,1)} %copy-done.38, bf16[160,2048]{1,0:T(8,128)(2,1)} %copy-done.40, bf16[160,1024]{1,0:T(8,128)(2,1)S(1)} %copy-done.25, bf16[160,1024]{1,0:T(8,128)(2,1)S(1)} %copy-done.22), kind=kOutput, calls=%fused_computation.128 | convolution fusion | flops 1355284480 | bytes 7471104 | tf_op jit(solution)/shard_map/rd,rf->df/dot_general | solution.py:33
  205.1 9.3 %all-to-all-start.3 = ((bf16[32,40,512]{2,1,0:T(8,128)(2,1)}), bf16[32,40,512]{2,1,0:T(8,128)(2,1)}, u32[]{:S(2)}, u32[]{:S(2)}) async-start(bf16[32,40,512]{2,1,0:T(8,128)(2,1)} %bitcast.17), calls=%async_computation.3 | async-start | bytes 2621440 | tf_op jit(solution)/shard_map/all_to_all | solution.py:106
  214.4 3.6 %fusion.48 = f32[1024,512]{1,0:T(8,128)} fusion(bf16[640,512]{1,0:T(8,128)(2,1)S(1)} %copy-done.20, bf16[160,1024]{1,0:T(8,128)(2,1)} %collective-permute-done.8, bf16[160,1024]{1,0:T(8,128)(2,1)} %collective-permute-done.7, bf16[160,1024]{1,0:T(8,128)(2,1)} %collective-permute-done.6, bf16[160,1024]{1,0:T(8,128)(2,1)} %multiply_convert_fusion.3), kind=kOutput, calls=%fused_computation.127 | convolution fusion | flops 676331520 | bytes 4063232 | tf_op jit(solution)/shard_map/rd,rf->df/dot_general | solution.py:33
  218.0 0.8 collective-permute-start.19
  219.0 1.5 copy.15
  220.5 1.7 multiply_reduce_fusion
  222.3 23.4 %psum.7 = f32[32,40]{1,0:T(8,128)S(1)} all-reduce(f32[32,40]{1,0:T(8,128)S(1)} %reshape.70), channel_id=1, replica_groups=mesh['dp'=32,'expert'=8] {'expert'}, use_global_device_ids=true, to_apply=%region_5.6 | all-reduce | flops 1280 | bytes 10240 | tf_op jit(solution)/shard_map/psum | solution.py:162
  246.0 0.6 divide_bitcast_fusion
  247.0 1.0 fusion.9
  248.1 4.1 %fusion.4 = bf16[1,1024,512]{2,1,0:T(8,128)(2,1)} fusion(f32[1024,512]{1,0:T(8,128)} %collective-permute-done.19, bf16[160,512]{1,0:T(8,128)(2,1)S(1)} %copy-done.13, bf16[160,512]{1,0:T(8,128)(2,1)S(1)} %copy-done.15, bf16[160,512]{1,0:T(8,128)(2,1)S(1)} %copy-done.17, bf16[160,512]{1,0:T(8,128)(2,1)S(1)} %copy-done.11, ...), kind=kOutput, calls=%fused_computation.13 | convolution fusion | flops 680001536 | bytes 5111808 | tf_op jit(solution)/shard_map/rd,rf->df/dot_general | solution.py:33
  252.2 2.4 fusion.8
  254.6 5.6 %fusion = bf16[1,512,2048]{2,1,0:T(8,128)(2,1)} fusion(f32[512,2048]{1,0:T(8,128)} %collective-permute-done.18, bf16[640,512]{1,0:T(8,128)(2,1)S(1)} %copy-done.18, bf16[160,2048]{1,0:T(8,128)(2,1)S(1)} %copy-done.37, bf16[160,2048]{1,0:T(8,128)(2,1)S(1)} %copy-done.39, bf16[160,2048]{1,0:T(8,128)(2,1)} %copy-done.40, bf16[160,1024]{1,0:T(8,128)(2,1)S(1)} %copy-done.26, ...), kind=kOutput, calls=%fused_computation.3 | convolution fusion | flops 1357381632 | bytes 9568256 | tf_op jit(solution)/shard_map/rd,rf->df/dot_general | solution.py:33
  (125 shorter events, 4.3 us)
Async XLA Ops:
  0.6 19.0 %copy-start = (bf16[128,512]{1,0:T(8,128)(2,1)S(1)}, bf16[128,512]{1,0:T(8,128)(2,1)}, u32[]{:S(2)}) copy-start(bf16[128,512]{1,0:T(8,128)(2,1)} %param.11) | copy-start | bytes 393220
  1.4 1.7 copy-start.33
  2.2 4.4 %copy-start.29 = (s32[1280]{0:T(1024)}, s32[1280]{0:T(1024)S(1)}, u32[]{:S(2)}) copy-start(s32[1280]{0:T(1024)S(1)} %eq.82) | copy-start | bytes 15364
  2.9 15.8 %copy-start.27 = (f32[32,128]{1,0:T(8,128)}, f32[32,128]{1,0:T(8,128)S(1)}, u32[]{:S(2)}) copy-start(f32[32,128]{1,0:T(8,128)S(1)} %get-tuple-element.24) | copy-start | bytes 49156
  4.0 13.3 %copy-start.2 = (bf16[1,512,2048]{2,1,0:T(8,128)(2,1)S(1)}, bf16[1,512,2048]{2,1,0:T(8,128)(2,1)}, u32[]{:S(2)}) copy-start(bf16[1,512,2048]{2,1,0:T(8,128)(2,1)} %param.9) | copy-start | bytes 6291460
  6.6 43.9 %all-to-all-start = ((bf16[32,40,512]{2,1,0:T(8,128)(2,1)}), bf16[32,40,512]{2,1,0:T(8,128)(2,1)}, u32[]{:S(2)}, u32[]{:S(2)}) async-start(bf16[32,40,512]{2,1,0:T(8,128)(2,1)} %bitcast.4), calls=%async_computation | async-start | bytes 2621440 | tf_op jit(solution)/shard_map/all_to_all | solution.py:106
  17.3 6.7 %collective-permute-start = (bf16[512,2048]{1,0:T(8,128)(2,1)S(1)}, bf16[512,2048]{1,0:T(8,128)(2,1)}, u32[]{:S(2)}, u32[]{:S(2)}) collective-permute-start(bf16[512,2048]{1,0:T(8,128)(2,1)S(1)} %bitcast.78), channel_id=1, source_target_pairs={{0,1},{1,0},{2,3},{3,2},{4,5},{5,4},{6,7},{7,6},{8,9},{9,8},{10,11... | collective-permute-start | bytes 6291464 | tf_op jit(solution)/shard_map/ppermute | solution.py:19
  18.6 5.4 %collective-permute-start.1 = (bf16[1024,512]{1,0:T(8,128)(2,1)}, bf16[1024,512]{1,0:T(8,128)(2,1)}, u32[]{:S(2)}, u32[]{:S(2)}) collective-permute-start(bf16[1024,512]{1,0:T(8,128)(2,1)} %bitcast.7), channel_id=1, source_target_pairs={{0,1},{1,0},{2,3},{3,2},{4,5},{5,4},{6,7},{7,6},{8,9},{9,8},{10,11... | collective-permute-start | bytes 3145736 | tf_op jit(solution)/shard_map/ppermute | solution.py:19
  53.6 10.6 %collective-permute-start.2 = (bf16[640,512]{1,0:T(8,128)(2,1)}, bf16[640,512]{1,0:T(8,128)(2,1)}, u32[]{:S(2)}, u32[]{:S(2)}) collective-permute-start(bf16[640,512]{1,0:T(8,128)(2,1)} %pad_maximum_fusion.2), channel_id=1, source_target_pairs={{0,1},{1,0},{2,3},{3,2},{4,5},{5,4},{6,7},{7,6},{8,9},{9,8},{10,11... | collective-permute-start | bytes 1966088 | tf_op jit(solution)/shard_map/ppermute | solution.py:19
  57.1 70.9 %all-to-all-start.2 = ((bf16[32,40,512]{2,1,0:T(8,128)(2,1)}), bf16[32,40,512]{2,1,0:T(8,128)(2,1)S(1)}, u32[]{:S(2)}, u32[]{:S(2)}) async-start(bf16[32,40,512]{2,1,0:T(8,128)(2,1)} %bitcast.80), calls=%async_computation.2 | async-start | bytes 2621440 | tf_op jit(solution)/shard_map/all_to_all | solution.py:106
  67.4 35.0 %copy-start.9 = (bf16[160,512]{1,0:T(8,128)(2,1)S(1)}, bf16[160,512]{1,0:T(8,128)(2,1)}, u32[]{:S(2)}) copy-start(bf16[160,512]{1,0:T(8,128)(2,1)} %get-tuple-element.45) | copy-start | bytes 491524
  67.4 30.2 %collective-permute-start.5 = (bf16[160,2048]{1,0:T(8,128)(2,1)S(1)}, bf16[160,2048]{1,0:T(8,128)(2,1)S(1)}, u32[]{:S(2)}, u32[]{:S(2)}) collective-permute-start(bf16[160,2048]{1,0:T(8,128)(2,1)S(1)} %get-tuple-element.28), channel_id=1, source_target_pairs={{0,6},{1,7},{2,0},{3,1},{4,2},{5,3},{6,4},{7,5},{8,14},{9,15},{10,... | collective-permute-start | bytes 1966088 | tf_op jit(solution)/shard_map/ppermute | solution.py:13
  70.2 27.4 %collective-permute-start.4 = (bf16[160,2048]{1,0:T(8,128)(2,1)S(1)}, bf16[160,2048]{1,0:T(8,128)(2,1)S(1)}, u32[]{:S(2)}, u32[]{:S(2)}) collective-permute-start(bf16[160,2048]{1,0:T(8,128)(2,1)S(1)} %get-tuple-element.29), channel_id=1, source_target_pairs={{0,4},{1,5},{2,6},{3,7},{4,0},{5,1},{6,2},{7,3},{8,12},{9,13},{10,... | collective-permute-start | bytes 1966088 | tf_op jit(solution)/shard_map/ppermute | solution.py:13
  70.6 31.9 %collective-permute-start.3 = (bf16[160,2048]{1,0:T(8,128)(2,1)S(1)}, bf16[160,2048]{1,0:T(8,128)(2,1)S(1)}, u32[]{:S(2)}, u32[]{:S(2)}) collective-permute-start(bf16[160,2048]{1,0:T(8,128)(2,1)S(1)} %get-tuple-element.27), channel_id=1, source_target_pairs={{0,2},{1,3},{2,4},{3,5},{4,6},{5,7},{6,0},{7,1},{8,10},{9,11},{10,... | collective-permute-start | bytes 1966088 | tf_op jit(solution)/shard_map/ppermute | solution.py:13
  103.3 1.1 copy-start.4
  105.3 17.3 %collective-permute-start.8 = (bf16[160,1024]{1,0:T(8,128)(2,1)}, bf16[160,1024]{1,0:T(8,128)(2,1)}, u32[]{:S(2)}, u32[]{:S(2)}) collective-permute-start(bf16[160,1024]{1,0:T(8,128)(2,1)} %multiply_convert_fusion.3), channel_id=1, source_target_pairs={{0,2},{1,3},{2,4},{3,5},{4,6},{5,7},{6,0},{7,1},{8,10},{9,11},{10,... | collective-permute-start | bytes 983048 | tf_op jit(solution)/shard_map/ppermute | solution.py:13
  105.3 17.3 %collective-permute-start.7 = (bf16[160,1024]{1,0:T(8,128)(2,1)}, bf16[160,1024]{1,0:T(8,128)(2,1)}, u32[]{:S(2)}, u32[]{:S(2)}) collective-permute-start(bf16[160,1024]{1,0:T(8,128)(2,1)} %multiply_convert_fusion.3), channel_id=1, source_target_pairs={{0,4},{1,5},{2,6},{3,7},{4,0},{5,1},{6,2},{7,3},{8,12},{9,13},{10,... | collective-permute-start | bytes 983048 | tf_op jit(solution)/shard_map/ppermute | solution.py:13
  105.7 17.3 %collective-permute-start.6 = (bf16[160,1024]{1,0:T(8,128)(2,1)}, bf16[160,1024]{1,0:T(8,128)(2,1)}, u32[]{:S(2)}, u32[]{:S(2)}) collective-permute-start(bf16[160,1024]{1,0:T(8,128)(2,1)} %multiply_convert_fusion.3), channel_id=1, source_target_pairs={{0,6},{1,7},{2,0},{3,1},{4,2},{5,3},{6,4},{7,5},{8,14},{9,15},{10,... | collective-permute-start | bytes 983048 | tf_op jit(solution)/shard_map/ppermute | solution.py:13
  126.4 13.0 %collective-permute-start.9 = (bf16[640,512]{1,0:T(8,128)(2,1)}, bf16[640,512]{1,0:T(8,128)(2,1)}, u32[]{:S(2)}, u32[]{:S(2)}) collective-permute-start(bf16[640,512]{1,0:T(8,128)(2,1)} %pad_maximum_fusion.3), channel_id=1, source_target_pairs={{0,1},{1,0},{2,3},{3,2},{4,5},{5,4},{6,7},{7,6},{8,9},{9,8},{10,11... | collective-permute-start | bytes 1966088 | tf_op jit(solution)/shard_map/ppermute | solution.py:19
  128.8 2.8 %copy-start.12 = (bf16[160,512]{1,0:T(8,128)(2,1)}, bf16[160,512]{1,0:T(8,128)(2,1)S(1)}, u32[]{:S(2)}) copy-start(bf16[160,512]{1,0:T(8,128)(2,1)S(1)} %get-tuple-element.31) | copy-start | bytes 491524
  128.8 2.8 %copy-start.14 = (bf16[160,512]{1,0:T(8,128)(2,1)}, bf16[160,512]{1,0:T(8,128)(2,1)S(1)}, u32[]{:S(2)}) copy-start(bf16[160,512]{1,0:T(8,128)(2,1)S(1)} %get-tuple-element.32) | copy-start | bytes 491524
  128.8 2.8 %copy-start.16 = (bf16[160,512]{1,0:T(8,128)(2,1)}, bf16[160,512]{1,0:T(8,128)(2,1)S(1)}, u32[]{:S(2)}) copy-start(bf16[160,512]{1,0:T(8,128)(2,1)S(1)} %get-tuple-element.33) | copy-start | bytes 491524
  128.8 4.7 %collective-permute-start.10 = (bf16[640,512]{1,0:T(8,128)(2,1)S(1)}, bf16[640,512]{1,0:T(8,128)(2,1)S(1)}, u32[]{:S(2)}, u32[]{:S(2)}) collective-permute-start(bf16[640,512]{1,0:T(8,128)(2,1)S(1)} %pad_maximum_fusion.4), channel_id=1, source_target_pairs={{0,1},{1,0},{2,3},{3,2},{4,5},{5,4},{6,7},{7,6},{8,9},{9,8},{10,11... | collective-permute-start | bytes 1966088 | tf_op jit(solution)/shard_map/ppermute | solution.py:19
  133.5 2.2 copy-start.19
  136.7 16.3 %collective-permute-start.13 = (bf16[160,1024]{1,0:T(8,128)(2,1)}, bf16[160,1024]{1,0:T(8,128)(2,1)}, u32[]{:S(2)}, u32[]{:S(2)}) collective-permute-start(bf16[160,1024]{1,0:T(8,128)(2,1)} %get-tuple-element.47), channel_id=1, source_target_pairs={{0,6},{1,7},{2,0},{3,1},{4,2},{5,3},{6,4},{7,5},{8,14},{9,15},{10,... | collective-permute-start | bytes 983048 | tf_op jit(solution)/shard_map/ppermute | solution.py:13
  138.8 14.3 %collective-permute-start.12 = (bf16[160,1024]{1,0:T(8,128)(2,1)}, bf16[160,1024]{1,0:T(8,128)(2,1)}, u32[]{:S(2)}, u32[]{:S(2)}) collective-permute-start(bf16[160,1024]{1,0:T(8,128)(2,1)} %get-tuple-element.48), channel_id=1, source_target_pairs={{0,4},{1,5},{2,6},{3,7},{4,0},{5,1},{6,2},{7,3},{8,12},{9,13},{10,... | collective-permute-start | bytes 983048 | tf_op jit(solution)/shard_map/ppermute | solution.py:13
  138.8 17.9 %collective-permute-start.11 = (bf16[160,1024]{1,0:T(8,128)(2,1)}, bf16[160,1024]{1,0:T(8,128)(2,1)}, u32[]{:S(2)}, u32[]{:S(2)}) collective-permute-start(bf16[160,1024]{1,0:T(8,128)(2,1)} %get-tuple-element.46), channel_id=1, source_target_pairs={{0,2},{1,3},{2,4},{3,5},{4,6},{5,7},{6,0},{7,1},{8,10},{9,11},{10,... | collective-permute-start | bytes 983048 | tf_op jit(solution)/shard_map/ppermute | solution.py:13
  141.9 57.4 %all-to-all-start.1 = ((bf16[32,40,512]{2,1,0:T(8,128)(2,1)}), bf16[32,40,512]{2,1,0:T(8,128)(2,1)S(1)}, u32[]{:S(2)}, u32[]{:S(2)}) async-start(bf16[32,40,512]{2,1,0:T(8,128)(2,1)} %bitcast.81), calls=%async_computation.1 | async-start | bytes 2621440 | tf_op jit(solution)/shard_map/all_to_all | solution.py:106
  153.0 9.2 %copy-start.5 = (bf16[160,512]{1,0:T(8,128)(2,1)S(1)}, bf16[160,512]{1,0:T(8,128)(2,1)}, u32[]{:S(2)}) copy-start(bf16[160,512]{1,0:T(8,128)(2,1)} %get-tuple-element.38) | copy-start | bytes 491524
  153.0 9.2 %copy-start.6 = (bf16[160,512]{1,0:T(8,128)(2,1)S(1)}, bf16[160,512]{1,0:T(8,128)(2,1)}, u32[]{:S(2)}) copy-start(bf16[160,512]{1,0:T(8,128)(2,1)} %get-tuple-element.39) | copy-start | bytes 491524
  153.0 9.2 %copy-start.7 = (bf16[160,512]{1,0:T(8,128)(2,1)S(1)}, bf16[160,512]{1,0:T(8,128)(2,1)}, u32[]{:S(2)}) copy-start(bf16[160,512]{1,0:T(8,128)(2,1)} %get-tuple-element.40) | copy-start | bytes 491524
  153.0 9.1 %copy-start.10 = (bf16[160,512]{1,0:T(8,128)(2,1)S(1)}, bf16[160,512]{1,0:T(8,128)(2,1)}, u32[]{:S(2)}) copy-start(bf16[160,512]{1,0:T(8,128)(2,1)} %get-tuple-element.45) | copy-start | bytes 491524
  159.3 37.0 %copy-start.21 = (bf16[160,1024]{1,0:T(8,128)(2,1)}, bf16[160,1024]{1,0:T(8,128)(2,1)S(1)}, u32[]{:S(2)}) copy-start(bf16[160,1024]{1,0:T(8,128)(2,1)S(1)} %get-tuple-element.25) | copy-start | bytes 983044
  159.3 37.0 %copy-start.24 = (bf16[160,1024]{1,0:T(8,128)(2,1)}, bf16[160,1024]{1,0:T(8,128)(2,1)S(1)}, u32[]{:S(2)}) copy-start(bf16[160,1024]{1,0:T(8,128)(2,1)S(1)} %get-tuple-element.26) | copy-start | bytes 983044
  159.4 30.8 %collective-permute-start.16 = (bf16[160,2048]{1,0:T(8,128)(2,1)S(1)}, bf16[160,2048]{1,0:T(8,128)(2,1)S(1)}, u32[]{:S(2)}, u32[]{:S(2)}) collective-permute-start(bf16[160,2048]{1,0:T(8,128)(2,1)S(1)} %pad_maximum_fusion.5), channel_id=1, source_target_pairs={{0,2},{1,3},{2,4},{3,5},{4,6},{5,7},{6,0},{7,1},{8,10},{9,11},{10,... | collective-permute-start | bytes 1966088 | tf_op jit(solution)/shard_map/ppermute | solution.py:13
  159.5 30.8 %collective-permute-start.15 = (bf16[160,2048]{1,0:T(8,128)(2,1)S(1)}, bf16[160,2048]{1,0:T(8,128)(2,1)S(1)}, u32[]{:S(2)}, u32[]{:S(2)}) collective-permute-start(bf16[160,2048]{1,0:T(8,128)(2,1)S(1)} %pad_maximum_fusion.5), channel_id=1, source_target_pairs={{0,4},{1,5},{2,6},{3,7},{4,0},{5,1},{6,2},{7,3},{8,12},{9,13},{10,... | collective-permute-start | bytes 1966088 | tf_op jit(solution)/shard_map/ppermute | solution.py:13
  160.5 30.1 %collective-permute-start.14 = (bf16[160,2048]{1,0:T(8,128)(2,1)S(1)}, bf16[160,2048]{1,0:T(8,128)(2,1)S(1)}, u32[]{:S(2)}, u32[]{:S(2)}) collective-permute-start(bf16[160,2048]{1,0:T(8,128)(2,1)S(1)} %pad_maximum_fusion.5), channel_id=1, source_target_pairs={{0,6},{1,7},{2,0},{3,1},{4,2},{5,3},{6,4},{7,5},{8,14},{9,15},{10,... | collective-permute-start | bytes 1966088 | tf_op jit(solution)/shard_map/ppermute | solution.py:13
  190.2 6.1 %copy-start.35 = (bf16[160,2048]{1,0:T(8,128)(2,1)}, bf16[160,2048]{1,0:T(8,128)(2,1)S(1)}, u32[]{:S(2)}) copy-start(bf16[160,2048]{1,0:T(8,128)(2,1)S(1)} %collective-permute-done.16) | copy-start | bytes 1966084
  190.2 6.1 %copy-start.38 = (bf16[160,2048]{1,0:T(8,128)(2,1)}, bf16[160,2048]{1,0:T(8,128)(2,1)S(1)}, u32[]{:S(2)}) copy-start(bf16[160,2048]{1,0:T(8,128)(2,1)S(1)} %collective-permute-done.15) | copy-start | bytes 1966084
  190.6 5.7 %copy-start.40 = (bf16[160,2048]{1,0:T(8,128)(2,1)}, bf16[160,2048]{1,0:T(8,128)(2,1)S(1)}, u32[]{:S(2)}) copy-start(bf16[160,2048]{1,0:T(8,128)(2,1)S(1)} %collective-permute-done.14) | copy-start | bytes 1966084
  194.2 3.8 %collective-permute-start.17 = (bf16[640,512]{1,0:T(8,128)(2,1)S(1)}, bf16[640,512]{1,0:T(8,128)(2,1)S(1)}, u32[]{:S(2)}, u32[]{:S(2)}) collective-permute-start(bf16[640,512]{1,0:T(8,128)(2,1)S(1)} %pad_maximum_fusion.6), channel_id=1, source_target_pairs={{0,1},{1,0},{2,3},{3,2},{4,5},{5,4},{6,7},{7,6},{8,9},{9,8},{10,11... | collective-permute-start | bytes 1966088 | tf_op jit(solution)/shard_map/ppermute | solution.py:19
  197.9 1.4 copy-start.22
  198.0 1.4 copy-start.25
  198.0 1.4 copy-start.36
  204.8 9.6 %copy-start.20 = (bf16[640,512]{1,0:T(8,128)(2,1)S(1)}, bf16[640,512]{1,0:T(8,128)(2,1)}, u32[]{:S(2)}) copy-start(bf16[640,512]{1,0:T(8,128)(2,1)} %copy-done.19) | copy-start | bytes 1966084
  204.8 49.8 %collective-permute-start.18 = (f32[512,2048]{1,0:T(8,128)}, f32[512,2048]{1,0:T(8,128)}, u32[]{:S(2)}, u32[]{:S(2)}) collective-permute-start(f32[512,2048]{1,0:T(8,128)} %fusion.49), channel_id=1, source_target_pairs={{0,1},{1,0},{2,3},{3,2},{4,5},{5,4},{6,7},{7,6},{8,9},{9,8},{10,11... | collective-permute-start | bytes 12582920 | tf_op jit(solution)/shard_map/ppermute | solution.py:19
  205.1 47.1 %all-to-all-start.3 = ((bf16[32,40,512]{2,1,0:T(8,128)(2,1)}), bf16[32,40,512]{2,1,0:T(8,128)(2,1)}, u32[]{:S(2)}, u32[]{:S(2)}) async-start(bf16[32,40,512]{2,1,0:T(8,128)(2,1)} %bitcast.17), calls=%async_computation.3 | async-start | bytes 2621440 | tf_op jit(solution)/shard_map/all_to_all | solution.py:106
  214.4 4.4 %copy-start.28 = (f32[32,128]{1,0:T(8,128)S(1)}, f32[32,128]{1,0:T(8,128)}, u32[]{:S(2)}) copy-start(f32[32,128]{1,0:T(8,128)} %copy-done.27) | copy-start | bytes 49156
  214.4 4.4 %copy-start.30 = (s32[1280]{0:T(1024)S(1)}, s32[1280]{0:T(1024)}, u32[]{:S(2)}) copy-start(s32[1280]{0:T(1024)} %copy-done.29) | copy-start | bytes 15364
  218.0 2.5 copy-start.3
  218.0 30.0 %collective-permute-start.19 = (f32[1024,512]{1,0:T(8,128)}, f32[1024,512]{1,0:T(8,128)}, u32[]{:S(2)}, u32[]{:S(2)}) collective-permute-start(f32[1024,512]{1,0:T(8,128)} %fusion.48), channel_id=1, source_target_pairs={{0,1},{1,0},{2,3},{3,2},{4,5},{5,4},{6,7},{7,6},{8,9},{9,8},{10,11... | collective-permute-start | bytes 6291464 | tf_op jit(solution)/shard_map/ppermute | solution.py:19
  220.5 25.4 %copy-start.32 = (s32[128,8]{0,1:T(8,128)S(1)}, s32[128,8]{0,1:T(8,128)}, u32[]{:S(2)}) copy-start(s32[128,8]{0,1:T(8,128)} %param.7) | copy-start | bytes 12292
  220.5 25.5 %copy-start.31 = (f32[128,8]{0,1:T(8,128)S(1)}, f32[128,8]{0,1:T(8,128)}, u32[]{:S(2)}) copy-start(f32[128,8]{0,1:T(8,128)} %param.8) | copy-start | bytes 12292
  220.5 25.5 %copy-start.34 = (f32[128]{0:T(128)S(1)}, f32[128]{0:T(128)}, u32[]{:S(2)}) copy-start(f32[128]{0:T(128)} %copy-done.33) | copy-start | bytes 1540
  246.6 1.4 copy-start.11
  246.6 1.5 copy-start.13
  246.6 1.5 copy-start.15
  246.6 1.5 copy-start.17
  248.0 6.6 %copy-start.18 = (bf16[640,512]{1,0:T(8,128)(2,1)S(1)}, bf16[640,512]{1,0:T(8,128)(2,1)}, u32[]{:S(2)}) copy-start(bf16[640,512]{1,0:T(8,128)(2,1)} %pad_maximum_fusion.7) | copy-start | bytes 1966084
  248.0 6.6 %copy-start.23 = (bf16[160,1024]{1,0:T(8,128)(2,1)S(1)}, bf16[160,1024]{1,0:T(8,128)(2,1)}, u32[]{:S(2)}) copy-start(bf16[160,1024]{1,0:T(8,128)(2,1)} %copy-done.21) | copy-start | bytes 983044
  248.0 6.6 %copy-start.26 = (bf16[160,1024]{1,0:T(8,128)(2,1)S(1)}, bf16[160,1024]{1,0:T(8,128)(2,1)}, u32[]{:S(2)}) copy-start(bf16[160,1024]{1,0:T(8,128)(2,1)} %copy-done.24) | copy-start | bytes 983044
  248.0 6.6 %copy-start.37 = (bf16[160,2048]{1,0:T(8,128)(2,1)S(1)}, bf16[160,2048]{1,0:T(8,128)(2,1)}, u32[]{:S(2)}) copy-start(bf16[160,2048]{1,0:T(8,128)(2,1)} %copy-done.35) | copy-start | bytes 1966084
  248.0 6.6 %copy-start.39 = (bf16[160,2048]{1,0:T(8,128)(2,1)S(1)}, bf16[160,2048]{1,0:T(8,128)(2,1)}, u32[]{:S(2)}) copy-start(bf16[160,2048]{1,0:T(8,128)(2,1)} %copy-done.38) | copy-start | bytes 1966084
  254.6 5.6 %copy-start.1 = (bf16[128,512]{1,0:T(8,128)(2,1)S(1)}, bf16[128,512]{1,0:T(8,128)(2,1)}, u32[]{:S(2)}) copy-start(bf16[128,512]{1,0:T(8,128)(2,1)} %param.11) | copy-start | bytes 393220
  (1 other events, 0.7 us)
where the time goes:
time: 265 us; the launch traced here: 260 us
  waiting for transfers between devices  103 us (39%)
  matrix products  54.5 us (21%)
  starting transfers between devices  54.2 us (20%)
  blocking collectives  23.4 us (9%)
  other arithmetic  13.2 us (5%)
  local copies, waits for them, and re-layouts  10.1 us (4%)
    ppermute x12, waiting for transfers between devices, permute_y(): lax.ppermute(v, 'expert', [(2 * y + c, 2 * ((y + step) % n_y) + c) for y...  75.2 us
    all_to_all x4, starting transfers between devices, exchange(): lax.all_to_all(v, 'dp', split_axis=0, concat_axis=0, tiled=True)  34 us
    all_to_all x4, waiting for transfers between devices, exchange(): lax.all_to_all(v, 'dp', split_axis=0, concat_axis=0, tiled=True)  26.5 us
    psum x1, blocking collectives, body(): slot_dot = lax.psum(slot_dot.reshape(n_data, capacity), 'expert')  23.4 us
    dot_general x7, matrix products, gather_dot(): return jnp.einsum('rd,rf->df', a, b, preferred_element_type=F32)  22.4 us
    dot_general x9, matrix products, dot(): return jnp.dot(a, b, preferred_element_type=F32)  18.6 us
    dot_general x6, matrix products, dot_t(): return jnp.einsum('rd,fd->rf', a, b, preferred_element_type=F32)  13.6 us
    ppermute x12, starting transfers between devices, permute_y(): lax.ppermute(v, 'expert', [(2 * y + c, 2 * ((y + step) % n_y) + c) for y...  11.9 us
  transfers between devices with their start and end apart: 24, of which 9 were waited for; matrix products, arithmetic and copies ran while one was open for 22% of the time, Pallas kernels for 0%

commit v1 on v0

--- a/solution.py
+++ b/solution.py
@@ -31,6 +31,10 @@
 
 def gather_dot(a, b):
     return jnp.einsum("rd,rf->df", a, b, preferred_element_type=F32)
+
+
+def permute_xor(v, bit, n_y):
+    return lax.ppermute(v, "expert", [(e, e ^ bit) for e in range(2 * n_y)])
 
 
 def reduce_rows(product, own, part, w_own, w_part, n_y):
@@ -86,11 +90,8 @@
 
     ids_t = expert_ids.T
     scores_t = scores.T
-    score_total = jnp.sum(scores_t, axis=0, keepdims=True)
-    weights_t = ROUTE_SCALE * scores_t / score_total
     named = ids_t[:, None, :] == jnp.arange(n_data, dtype=jnp.int32)[None, :, None]
     hot = jnp.sum(named.astype(F32), axis=0)
-    weight_of = jnp.sum(jnp.where(named, weights_t[:, None, :], 0.0), axis=0)
     before = (
         jnp.arange(tok_count, dtype=jnp.int32)[:, None] < jnp.arange(tok_count, dtype=jnp.int32)[None, :]
     ).astype(BF)
@@ -110,14 +111,14 @@
     in_part = permute_core(in_own, n_y)
     out_part = permute_core(out_own, n_y)
 
+    score_total = jnp.sum(scores_t, axis=0, keepdims=True)
+    weights_t = ROUTE_SCALE * scores_t / score_total
+    weight_of = jnp.sum(jnp.where(named, weights_t[:, None, :], 0.0), axis=0)
     weight_place = jnp.where(placed, weight_of[:, None, :], 0.0).reshape(slots, tok_count)
     row_weight = jnp.sum(weight_place, axis=1, keepdims=True)
     grad_rows = dot(place, out_grad)
     grad_send = (row_weight * grad_rows).astype(BF)
-    grad_rows = grad_rows.astype(BF)
-    token_slab, grad_send, in_part, out_part = lax.optimization_barrier(
-        (token_slab, grad_send, in_part, out_part)
-    )
+    grad_send, grad_rows = lax.optimization_barrier((grad_send, grad_rows.astype(BF)))
     grad_slab = exchange(grad_send)
 
     tok_part = permute_core(relative(token_slab, 1 - core, y, n_y), n_y)
@@ -145,7 +146,6 @@
     grad_other = permute_core(absolute(dot_t(gug, in_part).astype(BF), y, n_y), n_y)
     grad_mine = absolute(dot_t(gug, in_own).astype(BF), y, n_y)
     choice_grad = both_halves(grad_mine, grad_other, core)
-    out_back, choice_grad = lax.optimization_barrier((out_back, choice_grad))
     grad_back = exchange(choice_grad)
 
     tok_part, tok_own, _ = lax.optimization_barrier((tok_part, tok_own, choice_grad))
@@ -159,7 +159,11 @@
     high = high.astype(BF)
     layer_out = (gather_dot(high, out_back) + gather_dot(low, out_back)).astype(BF)
     slot_dot = jnp.sum(grad_rows.astype(F32) * out_back.astype(F32), axis=1)
-    slot_dot = lax.psum(slot_dot.reshape(n_data, capacity), "expert")
+    slot_dot = slot_dot.reshape(n_data, capacity)
+    bit = 1
+    while bit < 2 * n_y:
+        slot_dot = slot_dot + permute_xor(slot_dot, bit, n_y)
+        bit = 2 * bit
     dot_of = jnp.sum(jnp.where(placed, slot_dot[:, :, None], 0.0), axis=1)
     choice_dot = jnp.sum(jnp.where(named, dot_of[None, :, :], 0.0), axis=1)
     scores_grad = (

time: 265 us -> 253 us (0.955); the launches traced: 260 us -> 251 us
  blocking collectives: 23.4 us -> 0 us
  starting transfers between devices: 54.2 us -> 64.2 us
  waiting for transfers between devices: 103 us -> 112 us
  local copies, waits for them, and re-layouts: 10.1 us -> 4.89 us
    all_to_all x4, waiting for transfers between devices: 26.5 us -> 51.3 us  [exchange(): lax.all_to_all(v, 'dp', split_axis=0, concat_axis=0, tiled=True)]
    psum x1 -> x0, blocking collectives: 23.4 us -> none  [body(): slot_dot = lax.psum(slot_dot.reshape(n_data, capacity), 'expert')]
    ppermute x12, waiting for transfers between devices: 75.2 us -> 56.1 us  [permute_y(): lax.ppermute(v, 'expert', [(2 * y + c, 2 * ((y + step) % n_y) + c) for y...]
    ppermute x8, starting transfers between devices: 8.29 us -> 12.6 us  [permute_core(): lax.ppermute(v, 'expert', [(2 * y + c, 2 * y + 1 - c) for y in range(n_y)...]
    ppermute x0 -> x3, waiting for transfers between devices: none -> 3.73 us  [permute_xor(): return lax.ppermute(v, 'expert', [(e, e ^ bit) for e in range(2 * n_y)])]
    ppermute x0 -> x3, starting transfers between devices: none -> 3.43 us  [permute_xor(): return lax.ppermute(v, 'expert', [(e, e ^ bit) for e in range(2 * n_y)])]
    optimization_barrier x2 -> x0, local copies, waits for them, and re-layouts: 2.93 us -> none  [the longest x1 1.47 us: body(): lax.optimization_barrier((token_slab, grad_send, in_part, out_part))]
  transfers between devices with their start and end apart: 24 -> 27, of which waited for: 9 -> 15; matrix products, arithmetic and copies ran while one was open for 22% -> 25% of each run, Pallas kernels for 0% -> 0%
where the time goes in v1:
time: 253 us; the launch traced here: 251 us
  waiting for transfers between devices  112 us (44%)
  starting transfers between devices  64.2 us (25%)
  matrix products  57 us (23%)
  other arithmetic  11.7 us (5%)
  local copies, waits for them, and re-layouts  4.89 us (2%)
    ppermute x12, waiting for transfers between devices, permute_y(): lax.ppermute(v, 'expert', [(2 * y + c, 2 * ((y + step) % n_y) + c) for y...  56.1 us
    all_to_all x4, waiting for transfers between devices, exchange(): lax.all_to_all(v, 'dp', split_axis=0, concat_axis=0, tiled=True)  51.3 us
    all_to_all x4, starting transfers between devices, exchange(): lax.all_to_all(v, 'dp', split_axis=0, concat_axis=0, tiled=True)  34.2 us
    dot_general x7, matrix products, gather_dot(): return jnp.einsum('rd,rf->df', a, b, preferred_element_type=F32)  23.1 us
    dot_general x9, matrix products, dot(): return jnp.dot(a, b, preferred_element_type=F32)  19.3 us
    dot_general x6, matrix products, dot_t(): return jnp.einsum('rd,fd->rf', a, b, preferred_element_type=F32)  14.6 us
    ppermute x12, starting transfers between devices, permute_y(): lax.ppermute(v, 'expert', [(2 * y + c, 2 * ((y + step) % n_y) + c) for y...  13.9 us
    ppermute x8, starting transfers between devices, permute_core(): lax.ppermute(v, 'expert', [(2 * y + c, 2 * y + 1 - c) for y in range(n_y)...  12.6 us
  transfers between devices with their start and end apart: 27, of which 15 were waited for; matrix products, arithmetic and copies ran while one was open for 25% of the time, Pallas kernels for 0%

profile of v1, /device:TPU:33, one launch (start us, length us, event | category | flops | bytes accessed | tf_op | source)
XLA Modules:
  0.0 251.1 jit_solution(15838583148613615838)
XLA Ops:
  3.8 2.6 %convolution_convert_fusion = bf16[1280,512]{1,0:T(8,128)(2,1)} fusion(pred[1280,128]{1,0:T(32,128)(4,1)S(1)} %bitcast_compare_fusion, bf16[128,512]{1,0:T(8,128)(2,1)} %param.6), kind=kOutput, calls=%fused_computation.2 | convolution fusion | flops 168427520 | bytes 1605632 | tf_op jit(solution)/shard_map/dot_general | solution.py:25
  6.4 10.7 %all-to-all-start = ((bf16[32,40,512]{2,1,0:T(8,128)(2,1)}), bf16[32,40,512]{2,1,0:T(8,128)(2,1)}, u32[]{:S(2)}, u32[]{:S(2)}) async-start(bf16[32,40,512]{2,1,0:T(8,128)(2,1)} %bitcast.3), calls=%async_computation | async-start | bytes 2621440 | tf_op jit(solution)/shard_map/all_to_all | solution.py:107
  17.1 1.3 collective-permute-start.1
  18.9 31.5 %all-to-all-done = bf16[32,40,512]{2,1,0:T(8,128)(2,1)} async-done(((bf16[32,40,512]{2,1,0:T(8,128)(2,1)}), bf16[32,40,512]{2,1,0:T(8,128)(2,1)}, u32[]{:S(2)}, u32[]{:S(2)}) %all-to-all-start) | async-done | bytes 1310752 | tf_op jit(solution)/shard_map/all_to_all | solution.py:107
  50.3 2.3 constant_dynamic-slice_fusion.30
  52.6 0.9 pad_maximum_fusion.2
  53.5 2.0 collective-permute-start
  55.5 2.0 fusion.63
  57.4 4.9 %all-to-all-start.2 = ((bf16[32,40,512]{2,1,0:T(8,128)(2,1)}), bf16[32,40,512]{2,1,0:T(8,128)(2,1)S(1)}, u32[]{:S(2)}, u32[]{:S(2)}) async-start(bf16[32,40,512]{2,1,0:T(8,128)(2,1)} %bitcast.74), calls=%async_computation.2 | async-start | bytes 2621440 | tf_op jit(solution)/shard_map/all_to_all | solution.py:107
  62.3 2.3 fusion.24
  64.6 3.0 %add_convert_fusion.1 = bf16[480,2048]{1,0:T(8,128)(2,1)S(1)} fusion(f32[480,2048]{1,0:T(8,128)S(1)} %fusion.24, bf16[512,2048]{1,0:T(8,128)(2,1)} %collective-permute-done.1, bf16[640,512]{1,0:T(8,128)(2,1)} %collective-permute-done), kind=kOutput, calls=%fused_computation.1 | convolution fusion | flops 1008599040 | bytes 8486912 | tf_op jit(solution)/shard_map/dot_general | solution.py:25
  67.6 1.3 fusion.64
  69.0 1.3 collective-permute-start.2
  70.3 1.4 collective-permute-start.4
  71.7 1.6 collective-permute-start.3
  73.3 1.4 collective-permute-start.8
  74.7 2.0 pad_maximum_fusion.7
  76.8 1.4 fusion.57
  78.2 8.1 %collective-permute-done.2 = bf16[160,2048]{1,0:T(8,128)(2,1)} collective-permute-done((bf16[160,2048]{1,0:T(8,128)(2,1)}, bf16[160,2048]{1,0:T(8,128)(2,1)}, u32[]{:S(2)}, u32[]{:S(2)}) %collective-permute-start.2) | collective-permute-done | bytes 655392 | tf_op jit(solution)/shard_map/ppermute | solution.py:13
  86.3 15.2 %collective-permute-done.3 = bf16[160,2048]{1,0:T(8,128)(2,1)} collective-permute-done((bf16[160,2048]{1,0:T(8,128)(2,1)}, bf16[160,2048]{1,0:T(8,128)(2,1)}, u32[]{:S(2)}, u32[]{:S(2)}) %collective-permute-start.3) | collective-permute-done | bytes 655392 | tf_op jit(solution)/shard_map/ppermute | solution.py:13
  101.5 3.0 %fusion.4 = f32[160,2048]{1,0:T(8,128)S(1)} fusion(f32[160,2048]{1,0:T(8,128)S(1)} %fusion.57, bf16[512,2048]{1,0:T(8,128)(2,1)} %collective-permute-done.1, bf16[160,2048]{1,0:T(8,128)(2,1)} %collective-permute-done.4, bf16[160,2048]{1,0:T(8,128)(2,1)} %collective-permute-done.3, bf16[160,2048]{1,0:T(8,128)(2,1)} %collective-permute-done.2, ...), kind=kOutput, calls=%fused_computation.11 | convolution fusion | flops 337838080 | bytes 6848512 | tf_op jit(solution)/shard_map/dot_general | solution.py:25
  104.5 1.1 multiply_convert_fusion.3
  106.2 1.6 collective-permute-start.6
  107.8 0.8 collective-permute-start.5
  108.8 2.3 collective-permute-start.10
  111.1 1.9 fusion.30
  113.1 1.7 fusion.52
  114.8 1.1 collective-permute-done.7
  115.9 5.1 %collective-permute-done.6 = bf16[160,1024]{1,0:T(8,128)(2,1)} collective-permute-done((bf16[160,1024]{1,0:T(8,128)(2,1)}, bf16[160,1024]{1,0:T(8,128)(2,1)}, u32[]{:S(2)}, u32[]{:S(2)}) %collective-permute-start.6) | collective-permute-done | bytes 327712 | tf_op jit(solution)/shard_map/ppermute | solution.py:13
  121.0 2.3 collective-permute-done.5
  123.3 2.5 convolution_convert_fusion.3
  125.9 1.6 collective-permute-start.9
  127.6 2.2 add_convert_fusion.3
  130.2 2.4 collective-permute-start.13
  132.6 0.9 collective-permute-start.12
  133.4 2.5 convolution_convert_fusion.4
  135.9 4.4 %collective-permute-done.11 = bf16[160,1024]{1,0:T(8,128)(2,1)S(1)} collective-permute-done((bf16[160,1024]{1,0:T(8,128)(2,1)S(1)}, bf16[160,1024]{1,0:T(8,128)(2,1)S(1)}, u32[]{:S(2)}, u32[]{:S(2)}) %collective-permute-start.11) | collective-permute-done | bytes 327712 | tf_op jit(solution)/shard_map/ppermute | solution.py:13
  140.3 5.9 %collective-permute-done.13 = bf16[160,1024]{1,0:T(8,128)(2,1)S(1)} collective-permute-done((bf16[160,1024]{1,0:T(8,128)(2,1)S(1)}, bf16[160,1024]{1,0:T(8,128)(2,1)S(1)}, u32[]{:S(2)}, u32[]{:S(2)}) %collective-permute-start.13) | collective-permute-done | bytes 327712 | tf_op jit(solution)/shard_map/ppermute | solution.py:13
  146.2 2.0 collective-permute-done.12
  148.2 2.0 multiply_convert_fusion.2
  150.2 1.0 pad_maximum_fusion.5
  151.8 2.2 collective-permute-start.15
  154.3 1.3 maximum_select_fusion
  155.6 9.2 %all-to-all-start.1 = ((bf16[32,40,512]{2,1,0:T(8,128)(2,1)}), bf16[32,40,512]{2,1,0:T(8,128)(2,1)S(1)}, u32[]{:S(2)}, u32[]{:S(2)}) async-start(bf16[32,40,512]{2,1,0:T(8,128)(2,1)} %bitcast.76), calls=%async_computation.1 | async-start | bytes 2621440 | tf_op jit(solution)/shard_map/all_to_all | solution.py:107
  164.8 3.9 %fusion.61 = f32[1024,512]{1,0:T(8,128)} fusion(bf16[640,512]{1,0:T(8,128)(2,1)} %copy-done.15, bf16[160,1024]{1,0:T(8,128)(2,1)} %collective-permute-done.7, bf16[160,1024]{1,0:T(8,128)(2,1)} %collective-permute-done.6, bf16[160,1024]{1,0:T(8,128)(2,1)} %collective-permute-done.5, bf16[160,1024]{1,0:T(8,128)(2,1)} %multiply_convert_fusion.3), kind=kOutput, calls=%fused_computation.138 | convolution fusion | flops 676331520 | bytes 4063232 | tf_op jit(solution)/shard_map/rd,rf->df/dot_general | solution.py:33
  168.7 2.3 collective-permute-start.22
  171.0 11.0 %collective-permute-done.15 = bf16[160,2048]{1,0:T(8,128)(2,1)} collective-permute-done((bf16[160,2048]{1,0:T(8,128)(2,1)}, bf16[160,2048]{1,0:T(8,128)(2,1)}, u32[]{:S(2)}, u32[]{:S(2)}) %collective-permute-start.15) | collective-permute-done | bytes 655392 | tf_op jit(solution)/shard_map/ppermute | solution.py:13
  182.0 1.0 collective-permute-done.14
  183.0 5.5 %fusion.62 = f32[512,2048]{1,0:T(8,128)} fusion(bf16[640,512]{1,0:T(8,128)(2,1)} %collective-permute-done, bf16[160,2048]{1,0:T(8,128)(2,1)} %collective-permute-done.16, bf16[160,2048]{1,0:T(8,128)(2,1)} %collective-permute-done.15, bf16[160,2048]{1,0:T(8,128)(2,1)} %collective-permute-done.14, bf16[160,1024]{1,0:T(8,128)(2,1)S(1)} %copy-done.20, ...), kind=kOutput, calls=%fused_computation.139 | convolution fusion | flops 1355284480 | bytes 7471104 | tf_op jit(solution)/shard_map/rd,rf->df/dot_general | solution.py:33
  188.5 1.6 collective-permute-start.21
  190.1 3.8 %convolution_convert_fusion.1 = bf16[640,512]{1,0:T(8,128)(2,1)S(1)} fusion(bf16[512,2048]{1,0:T(8,128)(2,1)} %collective-permute-done.1, bf16[160,2048]{1,0:T(8,128)(2,1)} %collective-permute-done.16, bf16[160,2048]{1,0:T(8,128)(2,1)} %collective-permute-done.15, bf16[160,2048]{1,0:T(8,128)(2,1)} %collective-permute-done.14, ...), kind=kOutput, calls=%fused_computation.15 | convolution fusion | flops 1355612160 | bytes 5373952 | tf_op jit(solution)/shard_map/rd,fd->rf/dot_general | solution.py:29
  194.0 3.0 %convolution_convert_fusion.2 = bf16[640,512]{1,0:T(8,128)(2,1)S(1)} fusion(bf16[1,512,2048]{2,1,0:T(8,128)(2,1)S(1)} %copy-done.2, bf16[160,2048]{1,0:T(8,128)(2,1)} %collective-permute-done.16, bf16[160,2048]{1,0:T(8,128)(2,1)} %collective-permute-done.15, bf16[160,2048]{1,0:T(8,128)(2,1)} %collective-permute-done.14, ...), kind=kOutput, calls=%fused_computation.16 | convolution fusion | flops 1355612160 | bytes 5373952 | tf_op jit(solution)/shard_map/rd,fd->rf/dot_general | solution.py:29
  197.2 0.8 collective-permute-done.17
  198.0 1.3 maximum_select_fusion.1
  199.3 9.4 %all-to-all-start.3 = ((bf16[32,40,512]{2,1,0:T(8,128)(2,1)}), bf16[32,40,512]{2,1,0:T(8,128)(2,1)}, u32[]{:S(2)}, u32[]{:S(2)}) async-start(bf16[32,40,512]{2,1,0:T(8,128)(2,1)} %bitcast.75), calls=%async_computation.3 | async-start | bytes 2621440 | tf_op jit(solution)/shard_map/all_to_all | solution.py:107
  209.3 1.0 collective-permute-start.18
  210.3 4.0 %fusion.5 = bf16[1,1024,512]{2,1,0:T(8,128)(2,1)} fusion(f32[1024,512]{1,0:T(8,128)} %collective-permute-done.22, bf16[160,512]{1,0:T(8,128)(2,1)S(1)} %copy-done.9, bf16[160,512]{1,0:T(8,128)(2,1)S(1)} %copy-done.11, bf16[160,512]{1,0:T(8,128)(2,1)S(1)} %copy-done.13, bf16[160,512]{1,0:T(8,128)(2,1)S(1)} %copy-done.7, ...), kind=kOutput, calls=%fused_computation.14 | convolution fusion | flops 680001536 | bytes 5111808 | tf_op jit(solution)/shard_map/rd,rf->df/dot_general | solution.py:33
  215.1 2.3 collective-permute-done.19
  217.4 2.1 collective-permute-start.20
  219.5 1.0 fusion.11
  220.5 1.4 collective-permute-done.20
  222.9 19.8 %all-to-all-done.3 = bf16[32,40,512]{2,1,0:T(8,128)(2,1)} async-done(((bf16[32,40,512]{2,1,0:T(8,128)(2,1)}), bf16[32,40,512]{2,1,0:T(8,128)(2,1)}, u32[]{:S(2)}, u32[]{:S(2)}) %all-to-all-start.3) | async-done | bytes 1310752 | tf_op jit(solution)/shard_map/all_to_all | solution.py:107
  242.7 2.4 fusion.10
  245.1 6.0 %fusion = bf16[1,512,2048]{2,1,0:T(8,128)(2,1)} fusion(f32[512,2048]{1,0:T(8,128)} %collective-permute-done.21, bf16[640,512]{1,0:T(8,128)(2,1)S(1)} %copy-done.14, bf16[160,2048]{1,0:T(8,128)(2,1)} %collective-permute-done.16, bf16[160,2048]{1,0:T(8,128)(2,1)} %collective-permute-done.15, bf16[160,2048]{1,0:T(8,128)(2,1)} %collective-permute-done.14, ...), kind=kOutput, calls=%fused_computation.3 | convolution fusion | flops 1357381632 | bytes 9568256 | tf_op jit(solution)/shard_map/rd,rf->df/dot_general | solution.py:33
  (104 shorter events, 8.2 us)
Async XLA Ops:
  0.6 54.9 %copy-start = (bf16[128,512]{1,0:T(8,128)(2,1)S(1)}, bf16[128,512]{1,0:T(8,128)(2,1)}, u32[]{:S(2)}) copy-start(bf16[128,512]{1,0:T(8,128)(2,1)} %param.11) | copy-start | bytes 393220
  1.4 0.5 copy-start.26
  3.4 15.0 %copy-start.22 = (f32[32,128]{1,0:T(8,128)}, f32[32,128]{1,0:T(8,128)S(1)}, u32[]{:S(2)}) copy-start(f32[32,128]{1,0:T(8,128)S(1)} %get-tuple-element.15) | copy-start | bytes 49156
  3.8 13.3 %copy-start.2 = (bf16[1,512,2048]{2,1,0:T(8,128)(2,1)S(1)}, bf16[1,512,2048]{2,1,0:T(8,128)(2,1)}, u32[]{:S(2)}) copy-start(bf16[1,512,2048]{2,1,0:T(8,128)(2,1)} %param.9) | copy-start | bytes 6291460
  6.4 43.9 %all-to-all-start = ((bf16[32,40,512]{2,1,0:T(8,128)(2,1)}), bf16[32,40,512]{2,1,0:T(8,128)(2,1)}, u32[]{:S(2)}, u32[]{:S(2)}) async-start(bf16[32,40,512]{2,1,0:T(8,128)(2,1)} %bitcast.3), calls=%async_computation | async-start | bytes 2621440 | tf_op jit(solution)/shard_map/all_to_all | solution.py:107
  17.1 47.5 %collective-permute-start.1 = (bf16[512,2048]{1,0:T(8,128)(2,1)S(1)}, bf16[512,2048]{1,0:T(8,128)(2,1)}, u32[]{:S(2)}, u32[]{:S(2)}) collective-permute-start(bf16[512,2048]{1,0:T(8,128)(2,1)S(1)} %bitcast.72), channel_id=1, source_target_pairs={{0,1},{1,0},{2,3},{3,2},{4,5},{5,4},{6,7},{7,6},{8,9},{9,8},{10,11... | collective-permute-start | bytes 6291464 | tf_op jit(solution)/shard_map/ppermute | solution.py:19
  53.5 11.1 %collective-permute-start = (bf16[640,512]{1,0:T(8,128)(2,1)}, bf16[640,512]{1,0:T(8,128)(2,1)}, u32[]{:S(2)}, u32[]{:S(2)}) collective-permute-start(bf16[640,512]{1,0:T(8,128)(2,1)} %pad_maximum_fusion.2), channel_id=1, source_target_pairs={{0,1},{1,0},{2,3},{3,2},{4,5},{5,4},{6,7},{7,6},{8,9},{9,8},{10,11... | collective-permute-start | bytes 1966088 | tf_op jit(solution)/shard_map/ppermute | solution.py:19
  57.4 51.1 %all-to-all-start.2 = ((bf16[32,40,512]{2,1,0:T(8,128)(2,1)}), bf16[32,40,512]{2,1,0:T(8,128)(2,1)S(1)}, u32[]{:S(2)}, u32[]{:S(2)}) async-start(bf16[32,40,512]{2,1,0:T(8,128)(2,1)} %bitcast.74), calls=%async_computation.2 | async-start | bytes 2621440 | tf_op jit(solution)/shard_map/all_to_all | solution.py:107
  69.0 17.4 %collective-permute-start.2 = (bf16[160,2048]{1,0:T(8,128)(2,1)}, bf16[160,2048]{1,0:T(8,128)(2,1)}, u32[]{:S(2)}, u32[]{:S(2)}) collective-permute-start(bf16[160,2048]{1,0:T(8,128)(2,1)} %get-tuple-element.21), channel_id=1, source_target_pairs={{0,2},{1,3},{2,4},{3,5},{4,6},{5,7},{6,0},{7,1},{8,10},{9,11},{10,... | collective-permute-start | bytes 1966088 | tf_op jit(solution)/shard_map/ppermute | solution.py:13
  70.3 16.1 %collective-permute-start.4 = (bf16[160,2048]{1,0:T(8,128)(2,1)}, bf16[160,2048]{1,0:T(8,128)(2,1)}, u32[]{:S(2)}, u32[]{:S(2)}) collective-permute-start(bf16[160,2048]{1,0:T(8,128)(2,1)} %get-tuple-element.22), channel_id=1, source_target_pairs={{0,6},{1,7},{2,0},{3,1},{4,2},{5,3},{6,4},{7,5},{8,14},{9,15},{10,... | collective-permute-start | bytes 1966088 | tf_op jit(solution)/shard_map/ppermute | solution.py:13
  71.7 29.8 %collective-permute-start.3 = (bf16[160,2048]{1,0:T(8,128)(2,1)}, bf16[160,2048]{1,0:T(8,128)(2,1)}, u32[]{:S(2)}, u32[]{:S(2)}) collective-permute-start(bf16[160,2048]{1,0:T(8,128)(2,1)} %get-tuple-element.23), channel_id=1, source_target_pairs={{0,4},{1,5},{2,6},{3,7},{4,0},{5,1},{6,2},{7,3},{8,12},{9,13},{10,... | collective-permute-start | bytes 1966088 | tf_op jit(solution)/shard_map/ppermute | solution.py:13
  73.3 41.5 %collective-permute-start.8 = (bf16[1024,512]{1,0:T(8,128)(2,1)}, bf16[1024,512]{1,0:T(8,128)(2,1)}, u32[]{:S(2)}, u32[]{:S(2)}) collective-permute-start(bf16[1024,512]{1,0:T(8,128)(2,1)} %bitcast.6), channel_id=1, source_target_pairs={{0,1},{1,0},{2,3},{3,2},{4,5},{5,4},{6,7},{7,6},{8,9},{9,8},{10,11... | collective-permute-start | bytes 3145736 | tf_op jit(solution)/shard_map/ppermute | solution.py:19
  104.5 3.3 %copy-start.4 = (f32[160,2048]{1,0:T(8,128)}, f32[160,2048]{1,0:T(8,128)S(1)}, u32[]{:S(2)}) copy-start(f32[160,2048]{1,0:T(8,128)S(1)} %fusion.4) | copy-start | bytes 3932164
  105.6 10.3 %collective-permute-start.7 = (bf16[160,1024]{1,0:T(8,128)(2,1)}, bf16[160,1024]{1,0:T(8,128)(2,1)}, u32[]{:S(2)}, u32[]{:S(2)}) collective-permute-start(bf16[160,1024]{1,0:T(8,128)(2,1)} %multiply_convert_fusion.3), channel_id=1, source_target_pairs={{0,2},{1,3},{2,4},{3,5},{4,6},{5,7},{6,0},{7,1},{8,10},{9,11},{10,... | collective-permute-start | bytes 983048 | tf_op jit(solution)/shard_map/ppermute | solution.py:13
  106.2 14.9 %collective-permute-start.6 = (bf16[160,1024]{1,0:T(8,128)(2,1)}, bf16[160,1024]{1,0:T(8,128)(2,1)}, u32[]{:S(2)}, u32[]{:S(2)}) collective-permute-start(bf16[160,1024]{1,0:T(8,128)(2,1)} %multiply_convert_fusion.3), channel_id=1, source_target_pairs={{0,4},{1,5},{2,6},{3,7},{4,0},{5,1},{6,2},{7,3},{8,12},{9,13},{10,... | collective-permute-start | bytes 983048 | tf_op jit(solution)/shard_map/ppermute | solution.py:13
  107.8 15.5 %collective-permute-start.5 = (bf16[160,1024]{1,0:T(8,128)(2,1)}, bf16[160,1024]{1,0:T(8,128)(2,1)}, u32[]{:S(2)}, u32[]{:S(2)}) collective-permute-start(bf16[160,1024]{1,0:T(8,128)(2,1)} %multiply_convert_fusion.3), channel_id=1, source_target_pairs={{0,6},{1,7},{2,0},{3,1},{4,2},{5,3},{6,4},{7,5},{8,14},{9,15},{10,... | collective-permute-start | bytes 983048 | tf_op jit(solution)/shard_map/ppermute | solution.py:13
  108.7 4.4 %copy-start.8 = (bf16[160,512]{1,0:T(8,128)(2,1)}, bf16[160,512]{1,0:T(8,128)(2,1)S(1)}, u32[]{:S(2)}) copy-start(bf16[160,512]{1,0:T(8,128)(2,1)S(1)} %get-tuple-element.25) | copy-start | bytes 491524
  108.7 4.4 %copy-start.10 = (bf16[160,512]{1,0:T(8,128)(2,1)}, bf16[160,512]{1,0:T(8,128)(2,1)S(1)}, u32[]{:S(2)}) copy-start(bf16[160,512]{1,0:T(8,128)(2,1)S(1)} %get-tuple-element.26) | copy-start | bytes 491524
  108.7 4.4 %copy-start.12 = (bf16[160,512]{1,0:T(8,128)(2,1)}, bf16[160,512]{1,0:T(8,128)(2,1)S(1)}, u32[]{:S(2)}) copy-start(bf16[160,512]{1,0:T(8,128)(2,1)S(1)} %get-tuple-element.27) | copy-start | bytes 491524
  108.7 4.4 %copy-start.6 = (bf16[160,512]{1,0:T(8,128)(2,1)}, bf16[160,512]{1,0:T(8,128)(2,1)S(1)}, u32[]{:S(2)}) copy-start(bf16[160,512]{1,0:T(8,128)(2,1)S(1)} %get-tuple-element.31) | copy-start | bytes 491524
  108.8 18.8 %collective-permute-start.10 = (bf16[640,512]{1,0:T(8,128)(2,1)S(1)}, bf16[640,512]{1,0:T(8,128)(2,1)S(1)}, u32[]{:S(2)}, u32[]{:S(2)}) collective-permute-start(bf16[640,512]{1,0:T(8,128)(2,1)S(1)} %pad_maximum_fusion.4), channel_id=1, source_target_pairs={{0,1},{1,0},{2,3},{3,2},{4,5},{5,4},{6,7},{7,6},{8,9},{9,8},{10,11... | collective-permute-start | bytes 1966088 | tf_op jit(solution)/shard_map/ppermute | solution.py:19
  125.9 28.4 %collective-permute-start.9 = (bf16[640,512]{1,0:T(8,128)(2,1)S(1)}, bf16[640,512]{1,0:T(8,128)(2,1)S(1)}, u32[]{:S(2)}, u32[]{:S(2)}) collective-permute-start(bf16[640,512]{1,0:T(8,128)(2,1)S(1)} %pad_maximum_fusion.3), channel_id=1, source_target_pairs={{0,1},{1,0},{2,3},{3,2},{4,5},{5,4},{6,7},{7,6},{8,9},{9,8},{10,11... | collective-permute-start | bytes 1966088 | tf_op jit(solution)/shard_map/ppermute | solution.py:19
  127.6 20.7 %copy-start.15 = (bf16[640,512]{1,0:T(8,128)(2,1)}, bf16[640,512]{1,0:T(8,128)(2,1)S(1)}, u32[]{:S(2)}) copy-start(bf16[640,512]{1,0:T(8,128)(2,1)S(1)} %collective-permute-done.10) | copy-start | bytes 1966084
  129.8 10.5 %collective-permute-start.11 = (bf16[160,1024]{1,0:T(8,128)(2,1)S(1)}, bf16[160,1024]{1,0:T(8,128)(2,1)S(1)}, u32[]{:S(2)}, u32[]{:S(2)}) collective-permute-start(bf16[160,1024]{1,0:T(8,128)(2,1)S(1)} %get-tuple-element.40), channel_id=1, source_target_pairs={{0,2},{1,3},{2,4},{3,5},{4,6},{5,7},{6,0},{7,1},{8,10},{9,11},{10,... | collective-permute-start | bytes 983048 | tf_op jit(solution)/shard_map/ppermute | solution.py:13
  130.2 16.1 %collective-permute-start.13 = (bf16[160,1024]{1,0:T(8,128)(2,1)S(1)}, bf16[160,1024]{1,0:T(8,128)(2,1)S(1)}, u32[]{:S(2)}, u32[]{:S(2)}) collective-permute-start(bf16[160,1024]{1,0:T(8,128)(2,1)S(1)} %get-tuple-element.41), channel_id=1, source_target_pairs={{0,6},{1,7},{2,0},{3,1},{4,2},{5,3},{6,4},{7,5},{8,14},{9,15},{10,... | collective-permute-start | bytes 983048 | tf_op jit(solution)/shard_map/ppermute | solution.py:13
  132.6 15.7 %copy-start.5 = (f32[160,2048]{1,0:T(8,128)S(1)}, f32[160,2048]{1,0:T(8,128)}, u32[]{:S(2)}) copy-start(f32[160,2048]{1,0:T(8,128)} %copy-done.4) | copy-start | bytes 3932164
  132.6 15.7 %collective-permute-start.12 = (bf16[160,1024]{1,0:T(8,128)(2,1)S(1)}, bf16[160,1024]{1,0:T(8,128)(2,1)S(1)}, u32[]{:S(2)}, u32[]{:S(2)}) collective-permute-start(bf16[160,1024]{1,0:T(8,128)(2,1)S(1)} %get-tuple-element.42), channel_id=1, source_target_pairs={{0,4},{1,5},{2,6},{3,7},{4,0},{5,1},{6,2},{7,3},{8,12},{9,13},{10,... | collective-permute-start | bytes 983048 | tf_op jit(solution)/shard_map/ppermute | solution.py:13
  150.2 4.1 %copy-start.16 = (bf16[160,1024]{1,0:T(8,128)(2,1)}, bf16[160,1024]{1,0:T(8,128)(2,1)S(1)}, u32[]{:S(2)}) copy-start(bf16[160,1024]{1,0:T(8,128)(2,1)S(1)} %get-tuple-element.19) | copy-start | bytes 983044
  150.2 4.1 %copy-start.19 = (bf16[160,1024]{1,0:T(8,128)(2,1)}, bf16[160,1024]{1,0:T(8,128)(2,1)S(1)}, u32[]{:S(2)}) copy-start(bf16[160,1024]{1,0:T(8,128)(2,1)S(1)} %get-tuple-element.20) | copy-start | bytes 983044
  151.2 19.8 %collective-permute-start.16 = (bf16[160,2048]{1,0:T(8,128)(2,1)}, bf16[160,2048]{1,0:T(8,128)(2,1)}, u32[]{:S(2)}, u32[]{:S(2)}) collective-permute-start(bf16[160,2048]{1,0:T(8,128)(2,1)} %pad_maximum_fusion.5), channel_id=1, source_target_pairs={{0,2},{1,3},{2,4},{3,5},{4,6},{5,7},{6,0},{7,1},{8,10},{9,11},{10,... | collective-permute-start | bytes 1966088 | tf_op jit(solution)/shard_map/ppermute | solution.py:13
  151.8 30.2 %collective-permute-start.15 = (bf16[160,2048]{1,0:T(8,128)(2,1)}, bf16[160,2048]{1,0:T(8,128)(2,1)}, u32[]{:S(2)}, u32[]{:S(2)}) collective-permute-start(bf16[160,2048]{1,0:T(8,128)(2,1)} %pad_maximum_fusion.5), channel_id=1, source_target_pairs={{0,4},{1,5},{2,6},{3,7},{4,0},{5,1},{6,2},{7,3},{8,12},{9,13},{10,... | collective-permute-start | bytes 1966088 | tf_op jit(solution)/shard_map/ppermute | solution.py:13
  153.9 29.1 %collective-permute-start.14 = (bf16[160,2048]{1,0:T(8,128)(2,1)}, bf16[160,2048]{1,0:T(8,128)(2,1)}, u32[]{:S(2)}, u32[]{:S(2)}) collective-permute-start(bf16[160,2048]{1,0:T(8,128)(2,1)} %pad_maximum_fusion.5), channel_id=1, source_target_pairs={{0,6},{1,7},{2,0},{3,1},{4,2},{5,3},{6,4},{7,5},{8,14},{9,15},{10,... | collective-permute-start | bytes 1966088 | tf_op jit(solution)/shard_map/ppermute | solution.py:13
  155.6 43.7 %all-to-all-start.1 = ((bf16[32,40,512]{2,1,0:T(8,128)(2,1)}), bf16[32,40,512]{2,1,0:T(8,128)(2,1)S(1)}, u32[]{:S(2)}, u32[]{:S(2)}) async-start(bf16[32,40,512]{2,1,0:T(8,128)(2,1)} %bitcast.76), calls=%async_computation.1 | async-start | bytes 2621440 | tf_op jit(solution)/shard_map/all_to_all | solution.py:107
  164.8 18.2 %copy-start.17 = (bf16[160,1024]{1,0:T(8,128)(2,1)S(1)}, bf16[160,1024]{1,0:T(8,128)(2,1)}, u32[]{:S(2)}) copy-start(bf16[160,1024]{1,0:T(8,128)(2,1)} %copy-done.16) | copy-start | bytes 983044
  164.8 18.2 %copy-start.20 = (bf16[160,1024]{1,0:T(8,128)(2,1)S(1)}, bf16[160,1024]{1,0:T(8,128)(2,1)}, u32[]{:S(2)}) copy-start(bf16[160,1024]{1,0:T(8,128)(2,1)} %copy-done.19) | copy-start | bytes 983044
  168.7 41.6 %collective-permute-start.22 = (f32[1024,512]{1,0:T(8,128)}, f32[1024,512]{1,0:T(8,128)}, u32[]{:S(2)}, u32[]{:S(2)}) collective-permute-start(f32[1024,512]{1,0:T(8,128)} %fusion.61), channel_id=1, source_target_pairs={{0,1},{1,0},{2,3},{3,2},{4,5},{5,4},{6,7},{7,6},{8,9},{9,8},{10,11... | collective-permute-start | bytes 6291464 | tf_op jit(solution)/shard_map/ppermute | solution.py:19
  188.5 56.5 %collective-permute-start.21 = (f32[512,2048]{1,0:T(8,128)}, f32[512,2048]{1,0:T(8,128)}, u32[]{:S(2)}, u32[]{:S(2)}) collective-permute-start(f32[512,2048]{1,0:T(8,128)} %fusion.62), channel_id=1, source_target_pairs={{0,1},{1,0},{2,3},{3,2},{4,5},{5,4},{6,7},{7,6},{8,9},{9,8},{10,11... | collective-permute-start | bytes 12582920 | tf_op jit(solution)/shard_map/ppermute | solution.py:19
  193.9 4.1 %collective-permute-start.17 = (bf16[640,512]{1,0:T(8,128)(2,1)S(1)}, bf16[640,512]{1,0:T(8,128)(2,1)S(1)}, u32[]{:S(2)}, u32[]{:S(2)}) collective-permute-start(bf16[640,512]{1,0:T(8,128)(2,1)S(1)} %pad_maximum_fusion.6), channel_id=1, source_target_pairs={{0,1},{1,0},{2,3},{3,2},{4,5},{5,4},{6,7},{7,6},{8,9},{9,8},{10,11... | collective-permute-start | bytes 1966088 | tf_op jit(solution)/shard_map/ppermute | solution.py:19
  199.3 9.4 %copy-start.3 = (bf16[1280,512]{1,0:T(8,128)(2,1)S(1)}, bf16[1280,512]{1,0:T(8,128)(2,1)}, u32[]{:S(2)}) copy-start(bf16[1280,512]{1,0:T(8,128)(2,1)} %get-tuple-element.12) | copy-start | bytes 3932164
  199.3 43.4 %all-to-all-start.3 = ((bf16[32,40,512]{2,1,0:T(8,128)(2,1)}), bf16[32,40,512]{2,1,0:T(8,128)(2,1)}, u32[]{:S(2)}, u32[]{:S(2)}) async-start(bf16[32,40,512]{2,1,0:T(8,128)(2,1)} %bitcast.75), calls=%async_computation.3 | async-start | bytes 2621440 | tf_op jit(solution)/shard_map/all_to_all | solution.py:107
  208.7 1.6 copy-start.7
  208.7 1.6 copy-start.9
  208.7 1.6 copy-start.11
  208.7 1.6 copy-start.13
  209.2 5.4 %copy-start.23 = (f32[32,128]{1,0:T(8,128)S(1)}, f32[32,128]{1,0:T(8,128)}, u32[]{:S(2)}) copy-start(f32[32,128]{1,0:T(8,128)} %copy-done.22) | copy-start | bytes 49156
  209.3 5.1 %collective-permute-start.18 = (f32[32,40]{1,0:T(8,128)S(1)}, f32[32,40]{1,0:T(8,128)S(1)}, u32[]{:S(2)}, u32[]{:S(2)}) collective-permute-start(f32[32,40]{1,0:T(8,128)S(1)} %reshape.77), channel_id=1, source_target_pairs={{0,1},{1,0},{2,3},{3,2},{4,5},{5,4},{6,7},{7,6},{8,9},{9,8},{10,11... | collective-permute-start | bytes 15368 | tf_op jit(solution)/shard_map/ppermute | solution.py:37
  214.3 7.9 %copy-start.25 = (s32[128,8]{0,1:T(8,128)S(1)}, s32[128,8]{0,1:T(8,128)}, u32[]{:S(2)}) copy-start(s32[128,8]{0,1:T(8,128)} %param.7) | copy-start | bytes 12292
  214.3 7.9 %copy-start.24 = (f32[128,8]{0,1:T(8,128)S(1)}, f32[128,8]{0,1:T(8,128)}, u32[]{:S(2)}) copy-start(f32[128,8]{0,1:T(8,128)} %param.8) | copy-start | bytes 12292
  214.3 7.9 %copy-start.27 = (f32[128]{0:T(128)S(1)}, f32[128]{0:T(128)}, u32[]{:S(2)}) copy-start(f32[128]{0:T(128)} %copy-done.26) | copy-start | bytes 1540
  214.3 3.1 %collective-permute-start.19 = (f32[32,40]{1,0:T(8,128)S(1)}, f32[32,40]{1,0:T(8,128)S(1)}, u32[]{:S(2)}, u32[]{:S(2)}) collective-permute-start(f32[32,40]{1,0:T(8,128)S(1)} %add.253), channel_id=1, source_target_pairs={{0,2},{1,3},{2,0},{3,1},{4,6},{5,7},{6,4},{7,5},{8,10},{9,11},{10,... | collective-permute-start | bytes 15368 | tf_op jit(solution)/shard_map/ppermute | solution.py:37
  215.1 30.0 %copy-start.14 = (bf16[640,512]{1,0:T(8,128)(2,1)S(1)}, bf16[640,512]{1,0:T(8,128)(2,1)}, u32[]{:S(2)}) copy-start(bf16[640,512]{1,0:T(8,128)(2,1)} %pad_maximum_fusion.7) | copy-start | bytes 1966084
  215.1 30.0 %copy-start.18 = (bf16[160,1024]{1,0:T(8,128)(2,1)S(1)}, bf16[160,1024]{1,0:T(8,128)(2,1)}, u32[]{:S(2)}) copy-start(bf16[160,1024]{1,0:T(8,128)(2,1)} %copy-done.16) | copy-start | bytes 983044
  215.1 30.0 %copy-start.21 = (bf16[160,1024]{1,0:T(8,128)(2,1)S(1)}, bf16[160,1024]{1,0:T(8,128)(2,1)}, u32[]{:S(2)}) copy-start(bf16[160,1024]{1,0:T(8,128)(2,1)} %copy-done.19) | copy-start | bytes 983044
  217.4 4.5 %collective-permute-start.20 = (f32[32,40]{1,0:T(8,128)S(1)}, f32[32,40]{1,0:T(8,128)S(1)}, u32[]{:S(2)}, u32[]{:S(2)}) collective-permute-start(f32[32,40]{1,0:T(8,128)S(1)} %add.254), channel_id=1, source_target_pairs={{0,4},{1,5},{2,6},{3,7},{4,0},{5,1},{6,2},{7,3},{8,12},{9,13},{10,... | collective-permute-start | bytes 15368 | tf_op jit(solution)/shard_map/ppermute | solution.py:37
  245.1 6.0 %copy-start.1 = (bf16[128,512]{1,0:T(8,128)(2,1)S(1)}, bf16[128,512]{1,0:T(8,128)(2,1)}, u32[]{:S(2)}) copy-start(bf16[128,512]{1,0:T(8,128)(2,1)} %param.11) | copy-start | bytes 393220
